TPU v7x, 32 devices: a whole 2x2x4 slice. The times are simulated.
32 devices in a mesh: island: 2 (over x), row: 4 (over y, core), col: 4 (over z).
Axes of the slice: x: 2, y: 2, z: 4, core: 2. Of those that a mesh axis runs over, the one named last changes fastest.
Arguments:
- deltas: float32 [2, 4096, 8192], P('island', 'row', 'col'), may hold values from -0.13258252 to 0.13258252
- left_stat: float32 [4096, 4096], P(('island', 'col'), 'row'), may hold values from -1.5 to 1.5
- right_stat: float32 [8192, 8192], P(('island', 'row'), 'col'), may hold values from -1.5 to 1.5
Outputs:
- left_new: float32 [4096, 4096], P(('island', 'col'), 'row')
- right_new: float32 [8192, 8192], P(('island', 'row'), 'col')
All inputs are finite; a program needn't handle non-finite values.
Results may differ from a plain program's by a relative error of at most 0.00037.
Values may be sent and summed in bfloat16 or wider, within the bound.
A program may use at most 128 MiB of HBM per device.

v0:
```python
import jax
import jax.numpy as jnp
from jax import lax
from jax.sharding import PartitionSpec as P

M = 4096
N = 8192


def broadcast(value, axis, source):
    kept = jnp.where(lax.axis_index(axis) == source, value, 0).astype(value.dtype)
    return lax.psum(kept, axis)


def local(deltas, left_stat, right_stat):
    islands = lax.axis_size("island")
    row_count = lax.axis_size("row")
    island = lax.axis_index("island")
    local_delta = deltas[0]
    shares = lax.psum_scatter(local_delta, "island", scatter_dimension=0, tiled=True)
    rounded = (shares / islands).astype(jnp.bfloat16)
    panel = lax.all_gather(rounded, "island", axis=0, tiled=True)
    rows_local = panel.shape[0]
    rows_island = M // islands
    row_pieces = max(1, row_count // islands)
    row_extent = min(rows_island, rows_local)
    blocks = []
    for number in range(row_pieces):
        start_row = island * rows_island + number * row_extent
        source = start_row // rows_local
        blocks.append(broadcast(panel, "row", source))
    left_block = jnp.concatenate(blocks, axis=0)
    left_tile = lax.dot_general(
        left_block, panel, (((1,), (1,)), ((), ())), preferred_element_type=jnp.float32
    )
    left_shares = lax.psum_scatter(left_tile, "col", scatter_dimension=0, tiled=True)
    left_new = left_stat + left_shares
    cols_island = N // islands
    whole_rows = lax.all_gather(panel, "col", axis=1, tiled=True)
    right_block = lax.dynamic_slice_in_dim(whole_rows, island * cols_island, cols_island, 1)
    right_tile = lax.dot_general(
        right_block, panel, (((0,), (0,)), ((), ())), preferred_element_type=jnp.float32
    )
    right_shares = lax.psum_scatter(right_tile, "row", scatter_dimension=0, tiled=True)
    right_new = right_stat + right_shares
    return (left_new, right_new)


def solution(mesh):
    in_specs = (P("island", "row", "col"), P(("island", "col"), "row"), P(("island", "row"), "col"))
    out_specs = (P(("island", "col"), "row"), P(("island", "row"), "col"))
    return jax.shard_map(local, mesh=mesh, in_specs=in_specs, out_specs=out_specs, check_vma=False)
```

profile of v0, /device:TPU:0, one launch (start us, length us, event | category | flops | bytes accessed | tf_op | source)
XLA Modules:
  0.0 1020.4 jit_solution(15273571212736628576)
XLA Ops:
  7.2 0.0 reduce-scatter.4.cloned.1.call-start
  7.2 0.7 reduce-scatter.4.cloned.1.call-update
  7.9 0.0 all-gather.3.cloned.1.call-start
  7.9 104.4 %reduce-scatter.4.cloned.1.call-done = f32[512,2048]{1,0:T(8,128)} async-done(((f32[1024,2048]{1,0:T(8,128)}), f32[512,2048]{1,0:T(8,128)}) %reduce-scatter.4.cloned.1.call-update) | async-done | bytes 4194320 | tf_op jit(solution)/shard_map/reduce_scatter | solution.py:20
  112.3 4.0 multiply_convert_fusion
  116.3 0.0 all-gather.3.cloned.1.call-update
  116.4 0.0 all-reduce.3.cloned.1.call-start
  116.4 56.8 %all-gather.3.cloned.1.call-done = bf16[1024,2048]{1,0:T(8,128)(2,1)} async-done(((bf16[512,2048]{1,0:T(8,128)(2,1)}), bf16[1024,2048]{1,0:T(8,128)(2,1)}) %all-gather.3.cloned.1.call-update) | async-done | bytes 4194320 | tf_op jit(solution)/shard_map/all_gather | solution.py:22
  173.2 6.1 broadcast_select_fusion.1
  179.3 0.0 all-reduce.3.cloned.1.call-update
  179.4 0.0 all-gather.5.cloned.1.call-start
  179.4 0.5 all-gather.5.cloned.1.call-update
  179.9 0.0 reduce-scatter.6.cloned.1.call-start
  180.0 152.4 %all-reduce.3.cloned.1.call-done = (bf16[1024,2048]{1,0:T(8,128)(2,1)}, bf16[1024,2048]{1,0:T(8,128)(2,1)}) async-done(((bf16[1024,2048]{1,0:T(8,128)(2,1)}, bf16[1024,2048]{1,0:T(8,128)(2,1)}), (bf16[1024,2048]{1,0:T(8,128)(2,1)}, bf16[1024,2048]{1,0:T(8,128)(2,1)})) %all-reduce.3.cloned.1.call-update) | async-done | bytes 8388624 | tf_op jit(solution)/shard_map/psum | solution.py:12
  332.4 15.2 %fusion = f32[2048,1024]{1,0:T(8,128)} fusion(bf16[1024,2048]{1,0:T(8,128)(2,1)} %all-gather.3.cloned.1.call-done, bf16[1024,2048]{1,0:T(8,128)(2,1)} %get-tuple-element.2, bf16[1024,2048]{1,0:T(8,128)(2,1)} %get-tuple-element.3), kind=kOutput, calls=%fused_computation | convolution fusion | flops 8606711808 | bytes 20971520 | tf_op jit(solution)/shard_map/dot_general | solution.py:33
  347.6 0.0 reduce-scatter.6.cloned.1.call-update
  347.6 0.2 reduce-scatter.8.cloned.1.call-start
  347.9 272.9 %all-gather.5.cloned.1.call-done = bf16[1024,8192]{1,0:T(8,128)(2,1)} async-done(((bf16[1024,2048]{1,0:T(8,128)(2,1)}), bf16[1024,8192]{1,0:T(8,128)(2,1)}) %all-gather.5.cloned.1.call-update) | async-done | bytes 16777232 | tf_op jit(solution)/shard_map/all_gather | solution.py:39
  620.7 25.6 %fusion.4 = f32[4096,2048]{1,0:T(8,128)} fusion(bf16[1024,2048]{1,0:T(8,128)(2,1)} %all-gather.3.cloned.1.call-done, bf16[1024,8192]{1,0:T(8,128)(2,1)} %all-gather.5.cloned.1.call-done, s32[]{:T(128)S(6)} %select_n.31), kind=kOutput, calls=%fused_computation.4 | convolution fusion | flops 17179869184 | bytes 46137348 | tf_op jit(solution)/shard_map/dot_general | solution.py:41
  646.3 0.0 copy-start
  646.3 0.0 reduce-scatter.8.cloned.1.call-update
  646.3 120.0 %reduce-scatter.6.cloned.1.call-done = f32[512,1024]{1,0:T(8,128)} async-done(((f32[2048,1024]{1,0:T(8,128)}), f32[512,1024]{1,0:T(8,128)}) %reduce-scatter.6.cloned.1.call-update) | async-done | bytes 2097168 | tf_op jit(solution)/shard_map/reduce_scatter | solution.py:36
  766.3 0.0 copy-done
  766.3 3.3 add.25
  769.6 232.1 %reduce-scatter.8.cloned.1.call-done = f32[1024,2048]{1,0:T(8,128)} async-done(((f32[4096,2048]{1,0:T(8,128)}), f32[1024,2048]{1,0:T(8,128)}) %reduce-scatter.8.cloned.1.call-update) | async-done | bytes 8388624 | tf_op jit(solution)/shard_map/reduce_scatter | solution.py:44
  1001.7 11.9 %add.27 = f32[1024,2048]{1,0:T(8,128)} add(f32[1024,2048]{1,0:T(8,128)} %param.5, f32[1024,2048]{1,0:T(8,128)} %reduce-scatter.8.cloned.1.call-done) | non-fusion elementwise | flops 2097152 | bytes 25165824 | tf_op jit(solution)/shard_map/add | solution.py:45
Async XLA Ops:
  7.2 105.2 %reduce-scatter.4.cloned.1.call-start = ((), (), s32[]{:S(2)}) async-start(), calls=%async_computation.3 | async-start | bytes 12582912 | tf_op jit(solution)/shard_map/reduce_scatter | solution.py:20
  7.9 165.4 %all-gather.3.cloned.1.call-start = ((), (), s32[]{:S(2)}) async-start(), calls=%async_computation.4 | async-start | bytes 6291456 | tf_op jit(solution)/shard_map/all_gather | solution.py:22
  116.4 216.0 %all-reduce.3.cloned.1.call-start = ((), (), s32[]{:S(2)}) async-start(), calls=%async_computation.8 | async-start | bytes 16777216 | tf_op jit(solution)/shard_map/psum | solution.py:12
  179.4 441.4 %all-gather.5.cloned.1.call-start = ((), (), s32[]{:S(2)}) async-start(), calls=%async_computation.6 | async-start | bytes 20971520 | tf_op jit(solution)/shard_map/all_gather | solution.py:39
  179.9 586.4 %reduce-scatter.6.cloned.1.call-start = ((), (), s32[]{:S(2)}) async-start(), calls=%async_computation.5 | async-start | bytes 10485760 | tf_op jit(solution)/shard_map/reduce_scatter | solution.py:36
  347.6 654.1 %reduce-scatter.8.cloned.1.call-start = ((), (), s32[]{:S(2)}) async-start(), calls=%async_computation.7 | async-start | bytes 41943040 | tf_op jit(solution)/shard_map/reduce_scatter | solution.py:44
  646.3 120.1 %copy-start = (f32[512,1024]{1,0:T(8,128)S(1)}, f32[512,1024]{1,0:T(8,128)}, u32[]{:S(2)}) copy-start(f32[512,1024]{1,0:T(8,128)} %param.4) | copy-start | bytes 6291460
Sparse Core Ops, SparseCore 0:
  10.3 102.0 reduce-scatter.3
  116.5 56.7 all-gather.2
  179.5 152.8 all-reduce.2
  333.8 286.8 all-gather.4
  623.5 142.7 reduce-scatter.5
  768.8 232.9 reduce-scatter.7
where the time goes:
time: 1020 us
  waiting for transfers between devices  940 us (92%)
  matrix products  40.8 us (4%)
  other arithmetic  25.2 us (2%)
  between operations  14.1 us (1%)
    all_gather x1, waiting for transfers between devices, local(): whole_rows = lax.all_gather(panel, 'col', axis=1, tiled=True)  273 us
    reduce_scatter x1, waiting for transfers between devices, local(): lax.psum_scatter(right_tile, 'row', scatter_dimension=0, tiled=True)  232 us
    psum x1, waiting for transfers between devices, broadcast(): return lax.psum(kept, axis)  152 us
    reduce_scatter x1, waiting for transfers between devices, local(): lax.psum_scatter(left_tile, 'col', scatter_dimension=0, tiled=True)  120 us
    reduce_scatter x1, waiting for transfers between devices, local(): lax.psum_scatter(local_delta, 'island', scatter_dimension=0, tiled=True)  104 us
    all_gather x1, waiting for transfers between devices, local(): panel = lax.all_gather(rounded, 'island', axis=0, tiled=True)  56.8 us
    dot_general x1, matrix products, local(): lax.dot_general(right_block, panel, (((0,), (0,)), ((), ())), preferred_e...  25.6 us
  transfers between devices with their start and end apart: 6, of which 6 were waited for; matrix products, arithmetic and copies ran while one was open for 4% of the time, Pallas kernels for 0%

commit v1 on v0

v1 whole, which is shorter than its diff:
```python
import functools

import jax
import jax.numpy as jnp
from jax import lax
from jax.experimental import pallas as pl
from jax.experimental.pallas import tpu as pltpu
from jax.sharding import PartitionSpec as P

CHUNKS = 8
AHEAD = 2
MESH = pl.DeviceIdType.MESH


def gather_kernel(
    islands, rows, cols, chunks,
    delta_ref, strip_ref, block_ref,
    own_v, got_v, out_v, load_sem, store_sem, send_sem, recv_sem,
):
    i, r, c = lax.axis_index("island"), lax.axis_index("row"), lax.axis_index("col")
    step_rows = delta_ref.shape[1] // chunks
    width = block_ref.shape[2]
    per_strip = islands * rows // cols
    number = i * rows + r
    home, part = number // per_strip, number % per_strip
    x_peer = {"island": 1 - i}
    far_row = (r + 2) % 4
    core_row = r + 1 - 2 * (r % 2)
    y_peer, core_peer = {"row": far_row}, {"row": core_row}
    up, down = {"col": c + 1}, {"col": c - 1}
    has_up, has_down = c < cols - 1, c > 0
    hops = jnp.abs(c - home)
    lag = jnp.maximum(hops, 1)

    def at(j):
        return pl.ds(pl.multiple_of(j * step_rows, step_rows), step_rows)

    def remote(src, dst, flow, j, peer, arrival=None):
        return pltpu.make_async_remote_copy(
            src_ref=src, dst_ref=dst,
            send_sem=send_sem.at[flow, j],
            recv_sem=recv_sem.at[flow if arrival is None else arrival, j],
            device_id=peer, device_id_type=MESH,
        )

    def x_wide(j):
        return remote(delta_ref.at[1 - i, at(j)], got_v.at[j], 0, j, x_peer)

    def x_round(j, half):
        piece = strip_ref.at[2 * r + half, at(j)]
        return remote(piece, piece, 1, j, x_peer)

    def slabs(row, flow, j, peer):
        piece = strip_ref.at[pl.ds(2 * row, 2), at(j)]
        return remote(piece, piece, flow, j, peer)

    def columns(which):
        return pl.ds(pl.multiple_of(which * width, width), width)

    def z_core(j):
        other = per_strip - 1 - part
        return remote(strip_ref.at[:, at(j), columns(other)], block_ref.at[:, at(j)], 5, j, core_peer)

    def z_first(j, flow, peer):
        return remote(strip_ref.at[:, at(j), columns(part)], block_ref.at[:, at(j)], flow, j, peer, 5)

    def z_next(j, flow, peer):
        return remote(block_ref.at[:, at(j)], block_ref.at[:, at(j)], flow, j, peer, 5)

    barrier = pltpu.get_barrier_semaphore()
    for peer in (x_peer, y_peer, core_peer):
        pl.semaphore_signal(barrier, inc=1, device_id=peer, device_id_type=MESH)

    @pl.when(has_up)
    def _():
        pl.semaphore_signal(barrier, inc=1, device_id=up, device_id_type=MESH)

    @pl.when(has_down)
    def _():
        pl.semaphore_signal(barrier, inc=1, device_id=down, device_id_type=MESH)

    load = pltpu.make_async_copy(delta_ref.at[i], own_v, load_sem)
    load.start()
    pl.semaphore_wait(barrier, 3 + has_up.astype(jnp.int32) + has_down.astype(jnp.int32))
    for j in range(min(AHEAD, chunks)):
        x_wide(j).start()
    load.wait()

    def inside(j):
        return jnp.logical_and(j >= 0, j < chunks)

    def step(t, _):
        @pl.when(t < chunks)
        def _():
            x_wide(t).wait_recv()
            out_v[t] = ((own_v[at(t)] + got_v[t]) / islands).astype(jnp.bfloat16)
            store = pltpu.make_async_copy(out_v.at[t], strip_ref.at[2 * r + i, at(t)], store_sem)
            store.start()
            store.wait()
            x_round(t, i).start()

        @pl.when(t + AHEAD < chunks)
        def _():
            x_wide(t + AHEAD).start()

        @pl.when(inside(t - 1))
        def _():
            x_round(t - 1, 1 - i).wait_recv()
            slabs(r, 2, t - 1, y_peer).start()
            slabs(r, 3, t - 1, core_peer).start()

        @pl.when(inside(t - 2))
        def _():
            slabs(far_row, 2, t - 2, y_peer).wait_recv()
            slabs(far_row, 4, t - 2, core_peer).start()

        @pl.when(inside(t - 3))
        def _():
            slabs(core_row, 3, t - 3, core_peer).wait_recv()
            slabs((core_row + 2) % 4, 4, t - 3, core_peer).wait_recv()

            @pl.when(hops == 0)
            def _():
                z_core(t - 3).start()

                @pl.when(has_up)
                def _():
                    z_first(t - 3, 6, up).start()

                @pl.when(has_down)
                def _():
                    z_first(t - 3, 7, down).start()

        late = t - 3 - lag

        @pl.when(inside(late))
        def _():
            z_core(late).wait_recv()

            @pl.when(jnp.logical_and(c > home, has_up))
            def _():
                z_next(late, 6, up).start()

            @pl.when(jnp.logical_and(c < home, has_down))
            def _():
                z_next(late, 7, down).start()

        return 0

    lax.fori_loop(0, chunks + 2 + cols, step, 0)

    def finish(j, _):
        x_wide(j).wait_send()
        x_round(j, i).wait_send()
        slabs(r, 2, j, y_peer).wait_send()
        slabs(r, 3, j, core_peer).wait_send()
        slabs(far_row, 4, j, core_peer).wait_send()

        @pl.when(hops == 0)
        def _():
            z_core(j).wait_send()

        @pl.when(jnp.logical_and(c >= home, has_up))
        def _():
            z_next(j, 6, up).wait_send()

        @pl.when(jnp.logical_and(c <= home, has_down))
        def _():
            z_next(j, 7, down).wait_send()

        return 0

    lax.fori_loop(0, chunks, finish, 0)


def gather(delta, islands, rows, cols):
    share, wide = delta.shape[0] // islands, delta.shape[1]
    width = wide * cols // (islands * rows)
    step_rows = share // CHUNKS
    strip, block = pl.pallas_call(
        functools.partial(gather_kernel, islands, rows, cols, CHUNKS),
        out_shape=(
            jax.ShapeDtypeStruct((rows * islands, share, wide), jnp.bfloat16),
            jax.ShapeDtypeStruct((rows * islands, share, width), jnp.bfloat16),
        ),
        in_specs=[pl.BlockSpec(memory_space=pl.ANY)],
        out_specs=(pl.BlockSpec(memory_space=pl.ANY), pl.BlockSpec(memory_space=pl.ANY)),
        scratch_shapes=[
            pltpu.VMEM((share, wide), jnp.float32),
            pltpu.VMEM((CHUNKS, step_rows, wide), jnp.float32),
            pltpu.VMEM((CHUNKS, step_rows, wide), jnp.bfloat16),
            pltpu.SemaphoreType.DMA,
            pltpu.SemaphoreType.DMA,
            pltpu.SemaphoreType.DMA((8, CHUNKS)),
            pltpu.SemaphoreType.DMA((8, CHUNKS)),
        ],
        compiler_params=pltpu.CompilerParams(collective_id=0, has_side_effects=True),
    )(delta.reshape(islands, share, wide))
    return strip.reshape(-1, wide), block.reshape(-1, width)


def paired(deltas, left_stat, right_stat):
    islands, rows, cols = (lax.axis_size(name) for name in ("island", "row", "col"))
    c = lax.axis_index("col")
    strip, block = gather(deltas[0], islands, rows, cols)
    features = strip.shape[0]
    extent = left_stat.shape[0]
    plane = jnp.concatenate(
        [
            lax.dynamic_slice_in_dim(block, n * (features // islands) + c * extent, extent, 0)
            for n in range(islands)
        ],
        axis=0,
    )
    tall = features // rows
    tiles = [
        lax.dot_general(
            plane, block[n * tall:(n + 1) * tall], (((1,), (1,)), ((), ())),
            preferred_element_type=jnp.float32,
        )
        for n in range(rows)
    ]
    by_row = lax.psum_scatter(jnp.concatenate(tiles, axis=0), "row", scatter_dimension=0, tiled=True)
    left_new = left_stat + lax.psum_scatter(by_row, "island", scatter_dimension=0, tiled=True)
    right_new = right_stat + lax.dot_general(
        block, strip, (((0,), (0,)), ((), ())), preferred_element_type=jnp.float32
    )
    return left_new, right_new


def broadcast(value, axis, source):
    kept = jnp.where(lax.axis_index(axis) == source, value, 0).astype(value.dtype)
    return lax.psum(kept, axis)


def general(deltas, left_stat, right_stat):
    islands = lax.axis_size("island")
    row_count = lax.axis_size("row")
    island = lax.axis_index("island")
    local_delta = deltas[0]
    shares = lax.psum_scatter(local_delta, "island", scatter_dimension=0, tiled=True)
    rounded = (shares / islands).astype(jnp.bfloat16)
    panel = lax.all_gather(rounded, "island", axis=0, tiled=True)
    rows_local = panel.shape[0]
    rows_island = rows_local * row_count // islands
    row_pieces = max(1, row_count // islands)
    row_extent = min(rows_island, rows_local)
    blocks = []
    for number in range(row_pieces):
        start_row = island * rows_island + number * row_extent
        blocks.append(broadcast(panel, "row", start_row // rows_local))
    left_block = jnp.concatenate(blocks, axis=0)
    left_tile = lax.dot_general(
        left_block, panel, (((1,), (1,)), ((), ())), preferred_element_type=jnp.float32
    )
    left_shares = lax.psum_scatter(left_tile, "col", scatter_dimension=0, tiled=True)
    left_new = left_stat + left_shares
    cols_island = panel.shape[1] * lax.axis_size("col") // islands
    whole_rows = lax.all_gather(panel, "col", axis=1, tiled=True)
    right_block = lax.dynamic_slice_in_dim(whole_rows, island * cols_island, cols_island, 1)
    right_tile = lax.dot_general(
        right_block, panel, (((0,), (0,)), ((), ())), preferred_element_type=jnp.float32
    )
    right_shares = lax.psum_scatter(right_tile, "row", scatter_dimension=0, tiled=True)
    right_new = right_stat + right_shares
    return (left_new, right_new)


def solution(mesh):
    in_specs = (P("island", "row", "col"), P(("island", "col"), "row"), P(("island", "row"), "col"))
    out_specs = (P(("island", "col"), "row"), P(("island", "row"), "col"))
    sizes = mesh.shape
    fits = sizes["island"] == 2 and sizes["row"] == 4 and sizes["island"] * sizes["row"] == 2 * sizes["col"]
    local = paired if fits else general
    return jax.shard_map(local, mesh=mesh, in_specs=in_specs, out_specs=out_specs, check_vma=False)
```

time: 1020 us -> 516 us (0.51)
  waiting for transfers between devices: 940 us -> 200 us
  Pallas kernels: 0 us -> 248 us
  other arithmetic: 25.2 us -> 10.5 us
    all_gather x2 -> x0, waiting for transfers between devices: 330 us -> none  [the longest x1 273 us: local(): whole_rows = lax.all_gather(panel, 'col', axis=1, tiled=True)]
    reduce_scatter x3 -> x2, waiting for transfers between devices: 457 us -> 200 us  [the longest x1 169 us: paired(): lax.psum_scatter(jnp.concatenate(tiles, axis=0), 'row', scatter_dimension...]
    pallas_call x0 -> x1, Pallas kernels: none -> 248 us  [gather(): pl.pallas_call(functools.partial(gather_kernel, islands, rows, cols, CHUN...]
    psum x1 -> x0, waiting for transfers between devices: 152 us -> none  [broadcast(): return lax.psum(kept, axis)]
    add x2 -> x1, other arithmetic: 15.2 us -> 3.3 us  [paired(): left_stat + lax.psum_scatter(by_row, 'island', scatter_dimension=0, tiled...]
    dot_general x2 -> x5, matrix products: 40.8 us -> 34.6 us  [the longest x1 24.9 us: paired(): lax.dot_general(block, strip, (((0,), (0,)), ((), ())), preferred_element...]
  transfers between devices with their start and end apart: 6 -> 2, of which waited for: 6 -> 2; matrix products, arithmetic and copies ran while one was open for 4% -> 5% of each run, Pallas kernels for 0% -> 0%
where the time goes in v1:
time: 516 us
  Pallas kernels  248 us (48%)
  waiting for transfers between devices  200 us (39%)
  matrix products  34.6 us (7%)
  between operations  14.1 us (3%)
  other arithmetic  10.5 us (2%)
  local copies, waits for them, and re-layouts  7.99 us (2%)
    pallas_call x1, Pallas kernels, gather(): pl.pallas_call(functools.partial(gather_kernel, islands, rows, cols, CHUN...  248 us
    reduce_scatter x1, waiting for transfers between devices, paired(): lax.psum_scatter(jnp.concatenate(tiles, axis=0), 'row', scatter_dimension...  169 us
    reduce_scatter x1, waiting for transfers between devices, paired(): lax.psum_scatter(by_row, 'island', scatter_dimension=0, tiled=True)  31.8 us
    dot_general x1, matrix products, paired(): lax.dot_general(block, strip, (((0,), (0,)), ((), ())), preferred_element...  24.9 us
  transfers between devices with their start and end apart: 2, of which 2 were waited for; matrix products, arithmetic and copies ran while one was open for 5% of the time, Pallas kernels for 0%

profile of v1, /device:TPU:0, one launch (start us, length us, event | category | flops | bytes accessed | tf_op | source)
XLA Modules:
  0.0 515.7 jit_solution(8506184445275699858)
XLA Ops:
  7.2 0.0 reduce-scatter.3.cloned.1.call-start
  7.2 247.8 %shard_map.50 = (bf16[8,512,2048]{2,1,0:T(8,128)(2,1)}, bf16[8,512,1024]{2,1,0:T(8,128)(2,1)}) custom-call(f32[2,512,2048]{2,1,0:T(8,128)} %bitcast.15), custom_call_target="tpu_custom_call" | custom-call | tf_op jit(solution)/shard_map/pallas_call | solution.py:180
  255.0 5.8 %fusion.4 = (bf16[2,512,1024]{2,1,0:T(8,128)(2,1)}, bf16[2,512,1024]{2,1,0:T(8,128)(2,1)}, bf16[2,512,1024]{2,1,0:T(8,128)(2,1)}, bf16[2,512,1024]{2,1,0:T(8,128)(2,1)S(1)}) fusion(bf16[8,512,1024]{2,1,0:T(8,128)(2,1)} %get-tuple-element.4), kind=kLoop, calls=%fused_computation.9 | loop fusion | bytes 16777216 | tf_op jit(solution)/shard_map/slice | solution.py:218
  260.7 0.0 copy-start.3
  260.7 1.9 constant_dynamic-slice_fusion.1
  262.6 0.4 copy-done.3
  263.0 0.0 copy-start.2
  263.0 2.4 fusion
  265.3 0.0 copy-done.2
  265.4 0.0 copy-start.1
  265.4 2.4 fusion.3
  267.8 0.0 copy-done.1
  267.8 2.4 fusion.1
  270.2 2.4 fusion.2
  272.7 7.2 %pad_maximum_fusion = f32[4096,1024]{1,0:T(8,128)} fusion(f32[1024,1024]{1,0:T(8,128)S(1)} %fusion, f32[1024,1024]{1,0:T(8,128)S(1)} %fusion.1, f32[1024,1024]{1,0:T(8,128)S(1)} %fusion.2, f32[1024,1024]{1,0:T(8,128)S(1)} %fusion.3), kind=kLoop, calls=%fused_computation | loop fusion | flops 12582912 | bytes 33554432 | tf_op jit(solution)/shard_map/concatenate | solution.py:223
  279.9 0.0 reduce-scatter.3.cloned.1.call-update
  279.9 0.2 reduce-scatter.5.cloned.1.call-start
  280.1 168.7 %reduce-scatter.3.cloned.1.call-done = f32[1024,1024]{1,0:T(8,128)} async-done(((f32[4096,1024]{1,0:T(8,128)}), f32[1024,1024]{1,0:T(8,128)}) %reduce-scatter.3.cloned.1.call-update) | async-done | bytes 4194320 | tf_op jit(solution)/shard_map/reduce_scatter | solution.py:223
  448.8 0.0 reduce-scatter.5.cloned.1.call-update
  448.8 0.0 copy-start
  448.8 24.9 %bitcast_add_fusion = f32[1024,2048]{1,0:T(8,128)} fusion(f32[1024,2048]{1,0:T(8,128)} %param.5, bf16[8,512,1024]{2,1,0:T(8,128)(2,1)} %get-tuple-element.4, bf16[8,512,2048]{2,1,0:T(8,128)(2,1)} %get-tuple-element.5), kind=kOutput, calls=%fused_computation.1 | convolution fusion | flops 17181966336 | bytes 41943040 | tf_op jit(solution)/shard_map/dot_general | solution.py:225
  473.7 31.8 %reduce-scatter.5.cloned.1.call-done = f32[512,1024]{1,0:T(8,128)} async-done(((f32[1024,1024]{1,0:T(8,128)}), f32[512,1024]{1,0:T(8,128)}) %reduce-scatter.5.cloned.1.call-update) | async-done | bytes 2097168 | tf_op jit(solution)/shard_map/reduce_scatter | solution.py:224
  505.5 0.0 copy-done
  505.5 3.3 add.20
Async XLA Ops:
  7.2 441.6 %reduce-scatter.3.cloned.1.call-start = ((), (), s32[]{:S(2)}) async-start(), calls=%async_computation.2 | async-start | bytes 20971520 | tf_op jit(solution)/shard_map/reduce_scatter | solution.py:223
  260.7 2.2 copy-start.3
  263.0 2.4 copy-start.2
  265.4 2.4 copy-start.1
  279.9 225.6 %reduce-scatter.5.cloned.1.call-start = ((), (), s32[]{:S(2)}) async-start(), calls=%async_computation.3 | async-start | bytes 6291456 | tf_op jit(solution)/shard_map/reduce_scatter | solution.py:224
  448.8 56.7 %copy-start = (f32[512,1024]{1,0:T(8,128)S(1)}, f32[512,1024]{1,0:T(8,128)}, u32[]{:S(2)}) copy-start(f32[512,1024]{1,0:T(8,128)} %param.4) | copy-start | bytes 6291460
Sparse Core Ops, SparseCore 0:
  280.0 168.7 reduce-scatter.2
  451.1 54.3 reduce-scatter.4
